TPU v7x, 512 devices: a whole 4x8x8 slice. The times are simulated.
512 devices in a mesh: chain: 2 (over x_lo), slab: 128 (over x_hi, z, y), vis: 2 (over core).
Axes of the slice: x: 4 (x_hi: 2, x_lo: 2; x = x_hi * 2 + x_lo), y: 8, z: 8, core: 2. Of those that a mesh axis runs over, the one named last changes fastest.
Arguments:
- screens: float32 [4, 2048, 2048], P(('chain', 'vis'), 'slab'), parts along dimension 0, may hold values from -6 to 6
- image: float32 [4096, 2048], P(('chain', 'slab')), parts along dimension 0, may hold values from -6 to 6
- vis_row: int32 [32768], P('slab'), may hold values from 0 to 2047
- vis_block: int32 [32768, 1], P('slab'), may hold values from 0 to 127; in each aligned block of 256 rows (0 to 255, 256 to 511, ...) at most 6 rows name the same one
- vis_column: int32 [32768], P('slab'), may hold values from 0 to 7
- vis_real: float32 [32768], P('slab'), may hold values from -6 to 6
- vis_imag: float32 [32768], P('slab'), may hold values from -6 to 6
- vis_weight: float32 [32768], P('slab'), may hold values from 0.5 to 4
Outputs:
- screen_grad: float32 [4, 2048, 2048], P(('chain', 'vis'), 'slab'), parts along dimension 0
There are 2 independent parts, one for each index of `chain`. A program takes and returns all parts, laid end to end along the dimension named above; an argument that names none is the same for every part. Nothing has to cross between parts.
Inputs may be any that keep to these rules, and one draw needn't show every extreme that they name: `vis_block`: among the 256 visibilities of one index of slab, at most 6 name any one block; in every draw some block of some index holds exactly 6.
All inputs are finite; a program needn't handle non-finite values.
Results may differ from a plain program's by a relative error of at most 0.013.
Values may be sent and summed in bfloat16 or wider, within the bound.
No kernel may reach another device: no remote copies, remote signals or barrier semaphores. Data moves between devices by JAX's collectives and lax.ppermute only.
A program may use at most 64 MiB of HBM per device.

v0:
```python
import math
import jax
import jax.numpy as jnp
from jax import lax
from jax.sharding import PartitionSpec as P

refract = 1.0
rank_rows = 512
sample_rows = 256
table_rows = 256


def with_halo(cells, sides, width):
    for axis, dim in sides:
        count = lax.axis_size(axis)
        head = lax.slice_in_dim(cells, 0, width, axis=dim)
        tail = lax.slice_in_dim(cells, cells.shape[dim] - width, cells.shape[dim], axis=dim)
        cells = jnp.concatenate(
            [
                lax.ppermute(tail, axis, [(i, (i + 1) % count) for i in range(count)]),
                cells,
                lax.ppermute(head, axis, [((i + 1) % count, i) for i in range(count)]),
            ],
            axis=dim,
        )
    return cells


def twiddle(first, second, length):
    phase = (first[:, None] * second[None, :] % length).astype(jnp.float32) * (
        2.0 * math.pi / length
    )
    return (jnp.cos(phase).astype(jnp.bfloat16), jnp.sin(phase).astype(jnp.bfloat16))


def col_slope(field):
    return (
        8.0 * (jnp.roll(field, -1, -1) - jnp.roll(field, 1, -1))
        - (jnp.roll(field, -2, -1) - jnp.roll(field, 2, -1))
    ) / 12.0


def col_adjoint(field):
    return (
        8.0 * (jnp.roll(field, 1, -1) - jnp.roll(field, -1, -1))
        - (jnp.roll(field, 2, -1) - jnp.roll(field, -2, -1))
    ) / 12.0


def row_slope(padded, row_count):
    return (
        8.0 * (padded[..., 3 : row_count + 3, :] - padded[..., 1 : row_count + 1, :])
        - (padded[..., 4 : row_count + 4, :] - padded[..., 0:row_count, :])
    ) / 12.0


def row_adjoint(padded, row_count):
    return (
        8.0 * (padded[..., 1 : row_count + 1, :] - padded[..., 3 : row_count + 3, :])
        - (padded[..., 0:row_count, :] - padded[..., 4 : row_count + 4, :])
    ) / 12.0


def local(screens, image, vis_row, vis_block, vis_column, vis_real, vis_imag, vis_weight):
    walkers, row_count, grid_size = screens.shape
    slabs = lax.axis_size("slab")
    half_kx = grid_size // 2
    vis_count = vis_row.shape[0]
    capacity = 3 * vis_count // slabs
    unitary = 1.0 / math.sqrt(grid_size)
    positions = jnp.arange(grid_size, dtype=jnp.int32)
    highest = lax.Precision.HIGHEST
    stacked = jnp.concatenate([screens, image[None]], axis=0)
    padded = with_halo(stacked.astype(jnp.bfloat16), (("slab", 1),), 2).astype(stacked.dtype)
    slope_x = col_slope(stacked)
    slope_y = row_slope(padded, row_count)
    joined = image[None] + refract * (
        slope_x[:walkers] * slope_x[walkers][None] + slope_y[:walkers] * slope_y[walkers][None]
    )
    joined_bf = joined.astype(jnp.bfloat16)
    owner_slab = vis_block[:, 0]
    owned = half_kx // slabs
    step_kx = min(table_rows, half_kx)
    real_parts = []
    imag_parts = []
    for offset in range(0, half_kx, step_kx):
        cos_rows, sin_rows = twiddle(
            offset + jnp.arange(step_kx, dtype=jnp.int32), positions, grid_size
        )
        with_cos = jnp.einsum(
            "kc,wrc->wkr", cos_rows, joined_bf, preferred_element_type=jnp.float32
        )
        with_sin = jnp.einsum(
            "kc,wrc->wkr", sin_rows, joined_bf, preferred_element_type=jnp.float32
        )
        real_parts.append((unitary * with_cos).astype(jnp.bfloat16))
        imag_parts.append((-unitary * with_sin).astype(jnp.bfloat16))
    spectra = jnp.stack([jnp.concatenate(real_parts, 1), jnp.concatenate(imag_parts, 1)])
    columns = lax.all_to_all(spectra, "slab", split_axis=2, concat_axis=3, tiled=True)
    payload = jnp.stack(
        [(vis_column * grid_size + vis_row).astype(jnp.float32), vis_real, vis_imag, vis_weight]
    )
    rank_size = math.gcd(rank_rows, vis_count)
    lower = (jnp.arange(rank_size)[:, None] > jnp.arange(rank_size)[None, :]).astype(jnp.float32)
    owner_hot = (owner_slab[:, None] == jnp.arange(slabs, dtype=jnp.int32)[None, :]).astype(
        jnp.float32
    )

    def rank_step(seen, hot_rows):
        before = jnp.dot(lower, hot_rows, precision=highest) + seen[None, :]
        return (seen + jnp.sum(hot_rows, 0), jnp.sum(before * hot_rows, 1))

    _, ranks = lax.scan(
        rank_step,
        jnp.zeros((slabs,), jnp.float32),
        owner_hot.reshape(vis_count // rank_size, rank_size, slabs),
    )
    destination = owner_slab * capacity + ranks.reshape(vis_count).astype(jnp.int32)
    buckets = (
        jnp.zeros((4, slabs * capacity), jnp.float32)
        .at[:, destination]
        .set(payload)
        .reshape(4, slabs, capacity)
    )
    arrived = lax.all_to_all(buckets, "slab", split_axis=1, concat_axis=1, tiled=True).reshape(
        4, slabs * capacity
    )
    span = walkers * owned
    flat = columns.reshape(2 * span, grid_size)
    total_slots = slabs * capacity
    step_rows = math.gcd(sample_rows, total_slots)
    owned_ids = jnp.arange(owned, dtype=jnp.int32)
    zeros_grid = jnp.zeros((span, grid_size), jnp.float32)

    def sample_step(index, sums):
        block_data = lax.dynamic_slice_in_dim(arrived, index * step_rows, step_rows, 1)
        cell_code = block_data[0].astype(jnp.int32)
        row_freq = cell_code % grid_size
        col_freq = cell_code // grid_size
        cos_rows, sin_rows = twiddle(row_freq, positions, grid_size)
        with_cos = lax.dot_general(
            cos_rows, flat, (((1,), (1,)), ((), ())), preferred_element_type=jnp.float32
        ).reshape(step_rows, 2, walkers, owned)
        with_sin = lax.dot_general(
            sin_rows, flat, (((1,), (1,)), ((), ())), preferred_element_type=jnp.float32
        ).reshape(step_rows, 2, walkers, owned)
        chooser = (col_freq[:, None] == owned_ids[None, :]).astype(jnp.float32)
        model_real = unitary * jnp.sum((with_cos[:, 0] + with_sin[:, 1]) * chooser[:, None, :], -1)
        model_imag = unitary * jnp.sum((with_cos[:, 1] - with_sin[:, 0]) * chooser[:, None, :], -1)
        error_real = (block_data[3][:, None] * (model_real - block_data[1][:, None])).astype(
            jnp.bfloat16
        )
        error_imag = (block_data[3][:, None] * (model_imag - block_data[2][:, None])).astype(
            jnp.bfloat16
        )
        spread = jnp.concatenate(
            [
                (error_real[:, :, None] * chooser[:, None, :]).reshape(step_rows, span),
                (error_imag[:, :, None] * chooser[:, None, :]).reshape(step_rows, span),
            ],
            1,
        ).astype(jnp.bfloat16)
        back_cos = lax.dot_general(
            spread, cos_rows, (((0,), (0,)), ((), ())), preferred_element_type=jnp.float32
        )
        back_sin = lax.dot_general(
            spread, sin_rows, (((0,), (0,)), ((), ())), preferred_element_type=jnp.float32
        )
        return (
            sums[0] + back_cos[:span] - back_sin[span:],
            sums[1] + back_sin[:span] + back_cos[span:],
        )

    sum_real, sum_imag = lax.fori_loop(
        0, total_slots // step_rows, sample_step, (zeros_grid, zeros_grid)
    )
    adjoint = (
        (unitary * jnp.stack([sum_real, sum_imag]))
        .astype(jnp.bfloat16)
        .reshape(2, walkers, owned, grid_size)
    )
    returned = lax.all_to_all(adjoint, "slab", split_axis=3, concat_axis=2, tiled=True)
    gradient = jnp.zeros((walkers, row_count, grid_size), jnp.float32)
    for offset in range(0, half_kx, step_kx):
        cos_rows, sin_rows = twiddle(
            offset + jnp.arange(step_kx, dtype=jnp.int32), positions, grid_size
        )
        part_real = returned[0][:, offset : offset + step_kx, :]
        part_imag = returned[1][:, offset : offset + step_kx, :]
        gradient = gradient + jnp.einsum(
            "wkr,kc->wrc", part_real, cos_rows, preferred_element_type=jnp.float32
        )
        gradient = gradient - jnp.einsum(
            "wkr,kc->wrc", part_imag, sin_rows, preferred_element_type=jnp.float32
        )
    gradient = unitary * gradient
    push_x = refract * slope_x[walkers][None] * gradient
    push_y = refract * slope_y[walkers][None] * gradient
    padded_y = with_halo(push_y.astype(jnp.bfloat16), (("slab", 1),), 2).astype(push_y.dtype)
    return col_adjoint(push_x) + row_adjoint(padded_y, row_count)


def solution(mesh):
    in_specs = (
        P(("chain", "vis"), "slab", None),
        P(("chain", "slab"), None),
        P("slab"),
        P("slab", None),
        P("slab"),
        P("slab"),
        P("slab"),
        P("slab"),
    )
    out_specs = P(("chain", "vis"), "slab", None)
    return jax.shard_map(local, mesh=mesh, in_specs=in_specs, out_specs=out_specs, check_vma=False)
```

profile of v0, /device:TPU:2, one launch (start us, length us, event | category | flops | bytes accessed | tf_op | source)
XLA Modules:
  0.0 358.0 jit_solution(11313475501157636354)
XLA Ops:
  0.0 1.0 fusion.92
  1.0 3.5 collective-permute-start
  4.5 13.8 %collective-permute-start.1 = (bf16[2,2,2048]{2,1,0:T(2,128)(2,1)S(1)}, bf16[2,2,2048]{2,1,0:T(2,128)(2,1)S(1)}, u32[]{:S(2)}, u32[]{:S(2)}) collective-permute-start(bf16[2,2,2048]{2,1,0:T(2,128)(2,1)S(1)} %get-tuple-element.290), channel_id=1, source_target_pairs={{2,0},{4,2},{6,4},{8,6},{10,8},{12,10},{14,12},{16,14},{18,16},{20... | collective-permute-start | bytes 49160 | tf_op jit(solution)/shard_map/ppermute | solution.py:22
  18.4 1.0 fusion.70
  21.7 1.2 scatter_custom_fusion
  23.3 0.9 copy.53
  24.2 9.4 %all-to-all-start = ((f32[4,128,6]{2,0,1:T(4,128)}), f32[4,128,6]{2,0,1:T(4,128)S(1)}, u32[]{:S(2)}, u32[]{:S(2)}) async-start(f32[4,128,6]{2,0,1:T(4,128)} %copy.53), calls=%async_computation | async-start | bytes 524288 | tf_op jit(solution)/shard_map/all_to_all | solution.py:125
  34.5 8.8 %fusion.82 = bf16[1,256,16]{1,2,0:T(8,128)(2,1)S(1)} fusion(bf16[16,2048]{1,0:T(8,128)(2,1)S(1)} %fusion.111), kind=kOutput, calls=%fused_computation.142 | convolution fusion | flops 24649728 | bytes 73728 | tf_op jit(solution)/shard_map/kc,wrc->wkr/dot_general | solution.py:93
  43.3 8.1 %fusion.79 = bf16[1,256,16]{1,2,0:T(8,128)(2,1)S(1)} fusion(bf16[16,2048]{1,0:T(8,128)(2,1)S(1)} %fusion.111, s32[256]{0:T(256)S(1)} %iota_add_fusion), kind=kOutput, calls=%fused_computation.139 | convolution fusion | flops 24649728 | bytes 74752 | tf_op jit(solution)/shard_map/kc,wrc->wkr/dot_general | solution.py:93
  51.4 8.0 %fusion.83 = bf16[1,256,16]{1,2,0:T(8,128)(2,1)S(1)} fusion(bf16[16,2048]{1,0:T(8,128)(2,1)S(1)} %fusion.111, s32[256]{0:T(256)S(1)} %iota_add_fusion), kind=kOutput, calls=%fused_computation.143 | convolution fusion | flops 24649728 | bytes 74752 | tf_op jit(solution)/shard_map/kc,wrc->wkr/dot_general | solution.py:90
  59.4 8.6 %fusion.80 = bf16[1,256,16]{1,2,0:T(8,128)(2,1)S(1)} fusion(bf16[16,2048]{1,0:T(8,128)(2,1)S(1)} %fusion.111, s32[256]{0:T(256)S(1)} %iota_add_fusion.1), kind=kOutput, calls=%fused_computation.140 | convolution fusion | flops 24649728 | bytes 74752 | tf_op jit(solution)/shard_map/kc,wrc->wkr/dot_general | solution.py:93
  68.0 8.0 %fusion.84 = bf16[1,256,16]{1,2,0:T(8,128)(2,1)S(1)} fusion(bf16[16,2048]{1,0:T(8,128)(2,1)S(1)} %fusion.111, s32[256]{0:T(256)S(1)} %iota_add_fusion.1), kind=kOutput, calls=%fused_computation.144 | convolution fusion | flops 24649728 | bytes 74752 | tf_op jit(solution)/shard_map/kc,wrc->wkr/dot_general | solution.py:90
  76.0 8.3 %fusion.81 = bf16[1,256,16]{1,2,0:T(8,128)(2,1)S(1)} fusion(bf16[16,2048]{1,0:T(8,128)(2,1)S(1)} %fusion.111, s32[256]{0:T(256)S(1)} %iota_add_fusion.2), kind=kOutput, calls=%fused_computation.141 | convolution fusion | flops 24649728 | bytes 74752 | tf_op jit(solution)/shard_map/kc,wrc->wkr/dot_general | solution.py:93
  84.3 8.0 %fusion.85 = bf16[1,256,16]{1,2,0:T(8,128)(2,1)S(1)} fusion(bf16[16,2048]{1,0:T(8,128)(2,1)S(1)} %fusion.111, s32[256]{0:T(256)S(1)} %iota_add_fusion.2), kind=kOutput, calls=%fused_computation.145 | convolution fusion | flops 24649728 | bytes 74752 | tf_op jit(solution)/shard_map/kc,wrc->wkr/dot_general | solution.py:90
  92.3 8.7 %fusion.86 = bf16[1,256,16]{1,2,0:T(8,128)(2,1)S(1)} fusion(bf16[16,2048]{1,0:T(8,128)(2,1)S(1)} %fusion.111), kind=kOutput, calls=%fused_computation.146 | convolution fusion | flops 24649728 | bytes 73728 | tf_op jit(solution)/shard_map/kc,wrc->wkr/dot_general | solution.py:90
  101.5 1.0 reshape.696
  102.5 16.4 %all-to-all-start.1 = ((bf16[128,2,128]{2,1,0:T(2,128)(2,1)}), bf16[128,2,128]{2,1,0:T(2,128)(2,1)S(1)}, u32[]{:S(2)}, u32[]{:S(2)}) async-start(bf16[128,2,128]{2,1,0:T(2,128)(2,1)} %reshape.696), calls=%async_computation.1 | async-start | bytes 131072 | tf_op jit(solution)/shard_map/all_to_all | solution.py:99
  119.1 14.1 %all-to-all-done.1 = bf16[128,2,128]{2,1,0:T(2,128)(2,1)S(1)} async-done(((bf16[128,2,128]{2,1,0:T(2,128)(2,1)}), bf16[128,2,128]{2,1,0:T(2,128)(2,1)S(1)}, u32[]{:S(2)}, u32[]{:S(2)}) %all-to-all-start.1) | async-done | bytes 65568 | tf_op jit(solution)/shard_map/all_to_all | solution.py:99
  133.8 0.8 reshape.673
  134.6 120.4 %while.24 = (s32[]{:T(128)}, f32[8,2048]{1,0:T(8,128)S(1)}, f32[8,2048]{1,0:T(8,128)S(1)}, f32[4,768]{1,0:T(4,128)S(1)}, bf16[16,2048]{1,0:T(8,128)(2,1)S(1)}, /...) while((s32[]{:T(128)}, f32[8,2048]{1,0:T(8,128)S(1)}, ...), condition=%wide.region_5.6_spmd.clone.clone, body=%wide.region_2.5_spmd.clone.clone.sunk | while | flops 98724360 | bytes 1034473 | solution.py:174
  156.4 7.8 %fusion.213 = f32[256,16]{0,1:T(8,128)S(1)} fusion(bf16[16,2048]{1,0:T(8,128)(2,1)S(1)} %get-tuple-element.382, s32[256]{0:T(256)S(1)} %get-tuple-element.341), kind=kOutput, calls=%fused_computation.16.clone.1 | convolution fusion | flops 24641536 | bytes 82944 | tf_op jit(solution)/shard_map/while/body/eval_jaxpr/dot_general | solution.py:141
  164.3 7.9 %fusion.212 = f32[256,16]{0,1:T(8,128)S(1)} fusion(bf16[16,2048]{1,0:T(8,128)(2,1)S(1)} %get-tuple-element.382, s32[256]{0:T(256)S(1)} %get-tuple-element.341), kind=kOutput, calls=%fused_computation.18.clone.1 | convolution fusion | flops 24641536 | bytes 82944 | tf_op jit(solution)/shard_map/while/body/eval_jaxpr/dot_general | solution.py:144
  172.2 7.9 %fusion.218 = f32[16,2048]{1,0:T(8,128)S(1)} fusion(s32[256]{0:T(256)S(1)} %get-tuple-element.341, bf16[256,8]{0,1:T(8,128)(2,1)S(1)} %get-tuple-element.350, bf16[256,8]{0,1:T(8,128)(2,1)S(1)} %get-tuple-element.351), kind=kOutput, calls=%fused_computation.17.clone.1 | convolution fusion | flops 24657920 | bytes 140288 | tf_op jit(solution)/shard_map/while/body/eval_jaxpr/dot_general | solution.py:166
  180.1 7.8 %fusion.217 = f32[16,2048]{1,0:T(8,128)S(1)} fusion(s32[256]{0:T(256)S(1)} %get-tuple-element.341, bf16[256,8]{0,1:T(8,128)(2,1)S(1)} %get-tuple-element.350, bf16[256,8]{0,1:T(8,128)(2,1)S(1)} %get-tuple-element.351), kind=kOutput, calls=%fused_computation.15.clone.1 | convolution fusion | flops 24657920 | bytes 140288 | tf_op jit(solution)/shard_map/while/body/eval_jaxpr/dot_general | solution.py:163
  188.1 7.8 %fusion.213 = f32[256,16]{0,1:T(8,128)S(1)} fusion(bf16[16,2048]{1,0:T(8,128)(2,1)S(1)} %get-tuple-element.382, s32[256]{0:T(256)S(1)} %get-tuple-element.341), kind=kOutput, calls=%fused_computation.16.clone.1 | convolution fusion | flops 24641536 | bytes 82944 | tf_op jit(solution)/shard_map/while/body/eval_jaxpr/dot_general | solution.py:141
  195.9 7.9 %fusion.212 = f32[256,16]{0,1:T(8,128)S(1)} fusion(bf16[16,2048]{1,0:T(8,128)(2,1)S(1)} %get-tuple-element.382, s32[256]{0:T(256)S(1)} %get-tuple-element.341), kind=kOutput, calls=%fused_computation.18.clone.1 | convolution fusion | flops 24641536 | bytes 82944 | tf_op jit(solution)/shard_map/while/body/eval_jaxpr/dot_general | solution.py:144
  203.9 7.9 %fusion.218 = f32[16,2048]{1,0:T(8,128)S(1)} fusion(s32[256]{0:T(256)S(1)} %get-tuple-element.341, bf16[256,8]{0,1:T(8,128)(2,1)S(1)} %get-tuple-element.350, bf16[256,8]{0,1:T(8,128)(2,1)S(1)} %get-tuple-element.351), kind=kOutput, calls=%fused_computation.17.clone.1 | convolution fusion | flops 24657920 | bytes 140288 | tf_op jit(solution)/shard_map/while/body/eval_jaxpr/dot_general | solution.py:166
  211.8 7.8 %fusion.217 = f32[16,2048]{1,0:T(8,128)S(1)} fusion(s32[256]{0:T(256)S(1)} %get-tuple-element.341, bf16[256,8]{0,1:T(8,128)(2,1)S(1)} %get-tuple-element.350, bf16[256,8]{0,1:T(8,128)(2,1)S(1)} %get-tuple-element.351), kind=kOutput, calls=%fused_computation.15.clone.1 | convolution fusion | flops 24657920 | bytes 140288 | tf_op jit(solution)/shard_map/while/body/eval_jaxpr/dot_general | solution.py:163
  219.8 7.8 %fusion.213 = f32[256,16]{0,1:T(8,128)S(1)} fusion(bf16[16,2048]{1,0:T(8,128)(2,1)S(1)} %get-tuple-element.382, s32[256]{0:T(256)S(1)} %get-tuple-element.341), kind=kOutput, calls=%fused_computation.16.clone.1 | convolution fusion | flops 24641536 | bytes 82944 | tf_op jit(solution)/shard_map/while/body/eval_jaxpr/dot_general | solution.py:141
  227.6 7.9 %fusion.212 = f32[256,16]{0,1:T(8,128)S(1)} fusion(bf16[16,2048]{1,0:T(8,128)(2,1)S(1)} %get-tuple-element.382, s32[256]{0:T(256)S(1)} %get-tuple-element.341), kind=kOutput, calls=%fused_computation.18.clone.1 | convolution fusion | flops 24641536 | bytes 82944 | tf_op jit(solution)/shard_map/while/body/eval_jaxpr/dot_general | solution.py:144
  235.6 7.9 %fusion.218 = f32[16,2048]{1,0:T(8,128)S(1)} fusion(s32[256]{0:T(256)S(1)} %get-tuple-element.341, bf16[256,8]{0,1:T(8,128)(2,1)S(1)} %get-tuple-element.350, bf16[256,8]{0,1:T(8,128)(2,1)S(1)} %get-tuple-element.351), kind=kOutput, calls=%fused_computation.17.clone.1 | convolution fusion | flops 24657920 | bytes 140288 | tf_op jit(solution)/shard_map/while/body/eval_jaxpr/dot_general | solution.py:166
  243.4 7.8 %fusion.217 = f32[16,2048]{1,0:T(8,128)S(1)} fusion(s32[256]{0:T(256)S(1)} %get-tuple-element.341, bf16[256,8]{0,1:T(8,128)(2,1)S(1)} %get-tuple-element.350, bf16[256,8]{0,1:T(8,128)(2,1)S(1)} %get-tuple-element.351), kind=kOutput, calls=%fused_computation.15.clone.1 | convolution fusion | flops 24657920 | bytes 140288 | tf_op jit(solution)/shard_map/while/body/eval_jaxpr/dot_general | solution.py:163
  255.8 1.1 reshape.698
  256.8 19.9 %all_to_all.35 = bf16[128,2,128]{2,1,0:T(2,128)(2,1)S(1)} all-to-all(bf16[128,2,128]{2,1,0:T(2,128)(2,1)S(1)} %reshape.698), channel_id=1, replica_groups=mesh['chain'=2,'slab'=128,'vis'=2] {'slab'}, dimensions={0} | all-to-all | bytes 131072 | tf_op jit(solution)/shard_map/all_to_all | solution.py:182
  276.8 1.2 reshape.699
  278.0 1.4 copy.62
  279.8 7.7 %fusion.87 = f32[16,2048]{1,0:T(8,128)S(1)} fusion(bf16[1,1024,16]{2,1,0:T(8,128)(2,1)S(1)} %bitcast.176), kind=kOutput, calls=%fused_computation.147 | convolution fusion | flops 24641536 | bytes 196608 | tf_op jit(solution)/shard_map/wkr,kc->wrc/dot_general | solution.py:190
  287.5 8.2 %convolution_subtract_fusion.3 = f32[16,2048]{1,0:T(8,128)S(1)} fusion(f32[16,2048]{1,0:T(8,128)S(1)} %fusion.87, bf16[1,1024,16]{2,1,0:T(8,128)(2,1)S(1)} %bitcast.172), kind=kOutput, calls=%fused_computation.88 | convolution fusion | flops 24674304 | bytes 327680 | tf_op jit(solution)/shard_map/wkr,kc->wrc/dot_general | solution.py:193
  295.7 8.0 %convolution_add_fusion.2 = f32[16,2048]{1,0:T(8,128)S(1)} fusion(f32[16,2048]{1,0:T(8,128)S(1)} %convolution_subtract_fusion.3, s32[256]{0:T(256)S(1)} %iota_add_fusion.2, bf16[1,1024,16]{2,1,0:T(8,128)(2,1)S(1)} %bitcast.177), kind=kOutput, calls=%fused_computation.87 | convolution fusion | flops 24674304 | bytes 328704 | tf_op jit(solution)/shard_map/wkr,kc->wrc/dot_general | solution.py:190
  303.7 7.9 %convolution_subtract_fusion.2 = f32[16,2048]{1,0:T(8,128)S(1)} fusion(f32[16,2048]{1,0:T(8,128)S(1)} %convolution_add_fusion.2, s32[256]{0:T(256)S(1)} %iota_add_fusion.2, bf16[1,1024,16]{2,1,0:T(8,128)(2,1)S(1)} %bitcast.173), kind=kOutput, calls=%fused_computation.86 | convolution fusion | flops 24674304 | bytes 328704 | tf_op jit(solution)/shard_map/wkr,kc->wrc/dot_general | solution.py:193
  311.6 8.0 %convolution_add_fusion.1 = f32[16,2048]{1,0:T(8,128)S(1)} fusion(f32[16,2048]{1,0:T(8,128)S(1)} %convolution_subtract_fusion.2, s32[256]{0:T(256)S(1)} %iota_add_fusion.1, bf16[1,1024,16]{2,1,0:T(8,128)(2,1)S(1)} %bitcast.178), kind=kOutput, calls=%fused_computation.85 | convolution fusion | flops 24674304 | bytes 328704 | tf_op jit(solution)/shard_map/wkr,kc->wrc/dot_general | solution.py:190
  319.6 8.3 %convolution_subtract_fusion.1 = f32[16,2048]{1,0:T(8,128)S(1)} fusion(f32[16,2048]{1,0:T(8,128)S(1)} %convolution_add_fusion.1, s32[256]{0:T(256)S(1)} %iota_add_fusion.1, bf16[1,1024,16]{2,1,0:T(8,128)(2,1)S(1)} %bitcast.174), kind=kOutput, calls=%fused_computation.84 | convolution fusion | flops 24674304 | bytes 328704 | tf_op jit(solution)/shard_map/wkr,kc->wrc/dot_general | solution.py:193
  327.8 7.8 %convolution_add_fusion = f32[16,2048]{1,0:T(8,128)S(1)} fusion(f32[16,2048]{1,0:T(8,128)S(1)} %convolution_subtract_fusion.1, s32[256]{0:T(256)S(1)} %iota_add_fusion, bf16[1,1024,16]{2,1,0:T(8,128)(2,1)S(1)} %bitcast.179), kind=kOutput, calls=%fused_computation.83 | convolution fusion | flops 24674304 | bytes 328704 | tf_op jit(solution)/shard_map/wkr,kc->wrc/dot_general | solution.py:190
  335.6 8.1 %slice_multiply_fusion.2 = (f32[1,16,2048]{2,1,0:T(8,128)S(1)}, bf16[1,16,2048]{2,1,0:T(8,128)(2,1)S(1)}) fusion(f32[2,16,2048]{2,1,0:T(8,128)S(1)} %fusion.98, f32[2,16,2048]{2,1,0:T(8,128)S(1)} %fusion.94, f32[16,2048]{1,0:T(8,128)S(1)} %convolution_add_fusion, s32[256]{0:T(256)S(1)} %iota_add_fusion, bf16[1,1024,16]{2,1,0:T(8,128)(2,1)S(1)} %bitcast.175), kind=kOutput, calls=%fused_computation.206 | convolution fusion | flops 24805376 | bytes 656384 | tf_op jit(solution)/shard_map/wkr,kc->wrc/dot_general | solution.py:193
  344.0 2.5 collective-permute-start.2
  346.6 9.0 %collective-permute-start.3 = (bf16[1,2,2048]{2,1,0:T(2,128)(2,1)S(1)}, bf16[1,2,2048]{2,1,0:T(2,128)(2,1)S(1)}, u32[]{:S(2)}, u32[]{:S(2)}) collective-permute-start(bf16[1,2,2048]{2,1,0:T(2,128)(2,1)S(1)} %get-tuple-element.292), channel_id=1, source_target_pairs={{2,0},{4,2},{6,4},{8,6},{10,8},{12,10},{14,12},{16,14},{18,16},{20... | collective-permute-start | bytes 24584 | tf_op jit(solution)/shard_map/ppermute | solution.py:22
  355.7 1.3 collective-permute-done.3
  357.0 0.8 fusion.103
  (66 shorter events, 6.8 us)
Async XLA Ops:
  1.0 33.2 %collective-permute-start = (bf16[2,2,2048]{2,1,0:T(2,128)(2,1)S(1)}, bf16[2,2,2048]{2,1,0:T(2,128)(2,1)S(1)}, u32[]{:S(2)}, u32[]{:S(2)}) collective-permute-start(bf16[2,2,2048]{2,1,0:T(2,128)(2,1)S(1)} %get-tuple-element.289), channel_id=1, source_target_pairs={{0,2},{2,4},{4,6},{6,8},{8,10},{10,12},{12,14},{14,16},{16,18},{18... | collective-permute-start | bytes 49160 | tf_op jit(solution)/shard_map/ppermute | solution.py:20
  4.5 29.8 %collective-permute-start.1 = (bf16[2,2,2048]{2,1,0:T(2,128)(2,1)S(1)}, bf16[2,2,2048]{2,1,0:T(2,128)(2,1)S(1)}, u32[]{:S(2)}, u32[]{:S(2)}) collective-permute-start(bf16[2,2,2048]{2,1,0:T(2,128)(2,1)S(1)} %get-tuple-element.290), channel_id=1, source_target_pairs={{2,0},{4,2},{6,4},{8,6},{10,8},{12,10},{14,12},{16,14},{18,16},{20... | collective-permute-start | bytes 49160 | tf_op jit(solution)/shard_map/ppermute | solution.py:22
  21.6 11.9 %copy-start = (f32[16,2048]{1,0:T(8,128)S(1)}, f32[16,2048]{1,0:T(8,128)}, u32[]{:S(2)}) copy-start(f32[16,2048]{1,0:T(8,128)} %param.11) | copy-start | bytes 393220
  21.6 11.9 %copy-start.1 = (f32[1,16,2048]{2,1,0:T(8,128)S(1)}, f32[1,16,2048]{2,1,0:T(8,128)}, u32[]{:S(2)}) copy-start(f32[1,16,2048]{2,1,0:T(8,128)} %param.10) | copy-start | bytes 393220
  24.2 78.3 %all-to-all-start = ((f32[4,128,6]{2,0,1:T(4,128)}), f32[4,128,6]{2,0,1:T(4,128)S(1)}, u32[]{:S(2)}, u32[]{:S(2)}) async-start(f32[4,128,6]{2,0,1:T(4,128)} %copy.53), calls=%async_computation | async-start | bytes 524288 | tf_op jit(solution)/shard_map/all_to_all | solution.py:125
  102.5 30.8 %all-to-all-start.1 = ((bf16[128,2,128]{2,1,0:T(2,128)(2,1)}), bf16[128,2,128]{2,1,0:T(2,128)(2,1)S(1)}, u32[]{:S(2)}, u32[]{:S(2)}) async-start(bf16[128,2,128]{2,1,0:T(2,128)(2,1)} %reshape.696), calls=%async_computation.1 | async-start | bytes 131072 | tf_op jit(solution)/shard_map/all_to_all | solution.py:99
  344.0 11.7 %collective-permute-start.2 = (bf16[1,2,2048]{2,1,0:T(2,128)(2,1)S(1)}, bf16[1,2,2048]{2,1,0:T(2,128)(2,1)S(1)}, u32[]{:S(2)}, u32[]{:S(2)}) collective-permute-start(bf16[1,2,2048]{2,1,0:T(2,128)(2,1)S(1)} %get-tuple-element.291), channel_id=1, source_target_pairs={{0,2},{2,4},{4,6},{6,8},{8,10},{10,12},{12,14},{14,16},{16,18},{18... | collective-permute-start | bytes 24584 | tf_op jit(solution)/shard_map/ppermute | solution.py:20
  346.6 10.4 %collective-permute-start.3 = (bf16[1,2,2048]{2,1,0:T(2,128)(2,1)S(1)}, bf16[1,2,2048]{2,1,0:T(2,128)(2,1)S(1)}, u32[]{:S(2)}, u32[]{:S(2)}) collective-permute-start(bf16[1,2,2048]{2,1,0:T(2,128)(2,1)S(1)} %get-tuple-element.292), channel_id=1, source_target_pairs={{2,0},{4,2},{6,4},{8,6},{10,8},{12,10},{14,12},{16,14},{18,16},{20... | collective-permute-start | bytes 24584 | tf_op jit(solution)/shard_map/ppermute | solution.py:22
where the time goes:
time: 361 us; the launch traced here: 358 us
  matrix products  226 us (63%)
  starting transfers between devices  54.7 us (15%)
  loops' own time  25.6 us (7%)
  blocking collectives  19.9 us (6%)
  waiting for transfers between devices  15.4 us (4%)
  local copies, waits for them, and re-layouts  10.7 us (3%)
  other arithmetic  5.4 us (1%)
    dot_general x4, matrix products, local(): jnp.einsum('kc,wrc->wkr', sin_rows, joined_bf, preferred_element_type=jnp...  33.7 us
    dot_general x4, matrix products, local(): jnp.einsum('kc,wrc->wkr', cos_rows, joined_bf, preferred_element_type=jnp...  32.8 us
    dot_general x4, matrix products, local(): jnp.einsum('wkr,kc->wrc', part_imag, sin_rows, preferred_element_type=jnp...  32.4 us
    dot_general x4, matrix products, local(): jnp.einsum('wkr,kc->wrc', part_real, cos_rows, preferred_element_type=jnp...  31.5 us
    another operation x1, loops' own time, local(): lax.fori_loop(0, total_slots // step_rows, sample_step, (zeros_grid, zero...  25.6 us
    dot_general x3, matrix products, sample_step(): lax.dot_general(sin_rows, flat, (((1,), (1,)), ((), ())), preferred_eleme...  23.8 us
    dot_general x3, matrix products, sample_step(): lax.dot_general(spread, sin_rows, (((0,), (0,)), ((), ())), preferred_ele...  23.6 us
    dot_general x3, matrix products, sample_step(): lax.dot_general(cos_rows, flat, (((1,), (1,)), ((), ())), preferred_eleme...  23.5 us
  transfers between devices with their start and end apart: 6, of which 2 were waited for; matrix products, arithmetic and copies ran while one was open for 21% of the time, Pallas kernels for 0%

commit v1 on v0

--- a/solution.py
+++ b/solution.py
@@ -122,9 +122,10 @@
         .set(payload)
         .reshape(4, slabs, capacity)
     )
-    arrived = lax.all_to_all(buckets, "slab", split_axis=1, concat_axis=1, tiled=True).reshape(
-        4, slabs * capacity
-    )
+    arrived = jnp.concatenate(
+        lax.all_to_all(jnp.stack(jnp.split(buckets, lax.axis_size("slab"), axis=1)), "slab", 0, 0),
+        axis=1,
+    ).reshape(4, slabs * capacity)
     span = walkers * owned
     flat = columns.reshape(2 * span, grid_size)
     total_slots = slabs * capacity

time: 361 us -> 436 us (1.21)
  local copies, waits for them, and re-layouts: 10.7 us -> 84.3 us
    unnamed x8 -> x135, local copies, waits for them, and re-layouts: 3.58 us -> 77.2 us
  transfers between devices with their start and end apart: 6 -> 6, of which waited for: 2 -> 2; matrix products, arithmetic and copies ran while one was open for 21% -> 34% of each run, Pallas kernels for 0% -> 0%
where the time goes in v1:
time: 436 us; the launch traced here: 432 us
  matrix products  226 us (52%)
  local copies, waits for them, and re-layouts  84.3 us (19%)
  starting transfers between devices  54.7 us (13%)
  loops' own time  25.6 us (6%)
  blocking collectives  19.9 us (5%)
  waiting for transfers between devices  15.4 us (4%)
  other arithmetic  5.4 us (1%)
    unnamed x135, local copies, waits for them, and re-layouts  77.2 us
    dot_general x4, matrix products, local(): jnp.einsum('kc,wrc->wkr', sin_rows, joined_bf, preferred_element_type=jnp...  33.7 us
    dot_general x4, matrix products, local(): jnp.einsum('kc,wrc->wkr', cos_rows, joined_bf, preferred_element_type=jnp...  32.8 us
    dot_general x4, matrix products, local(): jnp.einsum('wkr,kc->wrc', part_imag, sin_rows, preferred_element_type=jnp...  32.4 us
    dot_general x4, matrix products, local(): jnp.einsum('wkr,kc->wrc', part_real, cos_rows, preferred_element_type=jnp...  31.5 us
    another operation x1, loops' own time, local(): lax.fori_loop(0, total_slots // step_rows, sample_step, (zeros_grid, zero...  25.6 us
    dot_general x3, matrix products, sample_step(): lax.dot_general(sin_rows, flat, (((1,), (1,)), ((), ())), preferred_eleme...  23.8 us
    dot_general x3, matrix products, sample_step(): lax.dot_general(spread, sin_rows, (((0,), (0,)), ((), ())), preferred_ele...  23.6 us
  transfers between devices with their start and end apart: 6, of which 2 were waited for; matrix products, arithmetic and copies ran while one was open for 34% of the time, Pallas kernels for 0%

profile of v1, /device:TPU:2, one launch (start us, length us, event | category | flops | bytes accessed | tf_op | source)
XLA Modules:
  0.0 431.7 jit_solution(9069171801829583658)
XLA Ops:
  0.0 1.0 fusion.92
  1.0 3.5 collective-permute-start
  4.5 13.8 %collective-permute-start.1 = (bf16[2,2,2048]{2,1,0:T(2,128)(2,1)S(1)}, bf16[2,2,2048]{2,1,0:T(2,128)(2,1)S(1)}, u32[]{:S(2)}, u32[]{:S(2)}) collective-permute-start(bf16[2,2,2048]{2,1,0:T(2,128)(2,1)S(1)} %get-tuple-element.418), channel_id=1, source_target_pairs={{2,0},{4,2},{6,4},{8,6},{10,8},{12,10},{14,12},{16,14},{18,16},{20... | collective-permute-start | bytes 49160 | tf_op jit(solution)/shard_map/ppermute | solution.py:22
  18.4 1.0 fusion.70
  21.6 1.3 scatter_custom_fusion
  97.9 9.4 %all-to-all-start = ((f32[128,4,1,6]{3,1,2,0:T(4,128)}), f32[128,4,1,6]{3,1,2,0:T(4,128)S(1)}, u32[]{:S(2)}, u32[]{:S(2)}) async-start(f32[128,4,1,6]{3,1,2,0:T(4,128)} %constant_dynamic-update-slice_fusion), calls=%async_computation | async-start | bytes 524288 | tf_op jit(solution)/shard_map/all_to_all | solution.py:126
  108.2 8.8 %fusion.82 = bf16[1,256,16]{1,2,0:T(8,128)(2,1)S(1)} fusion(bf16[16,2048]{1,0:T(8,128)(2,1)S(1)} %fusion.111), kind=kOutput, calls=%fused_computation.142 | convolution fusion | flops 24649728 | bytes 73728 | tf_op jit(solution)/shard_map/kc,wrc->wkr/dot_general | solution.py:93
  117.0 8.1 %fusion.79 = bf16[1,256,16]{1,2,0:T(8,128)(2,1)S(1)} fusion(bf16[16,2048]{1,0:T(8,128)(2,1)S(1)} %fusion.111, s32[256]{0:T(256)S(1)} %iota_add_fusion), kind=kOutput, calls=%fused_computation.139 | convolution fusion | flops 24649728 | bytes 74752 | tf_op jit(solution)/shard_map/kc,wrc->wkr/dot_general | solution.py:93
  125.1 8.0 %fusion.83 = bf16[1,256,16]{1,2,0:T(8,128)(2,1)S(1)} fusion(bf16[16,2048]{1,0:T(8,128)(2,1)S(1)} %fusion.111, s32[256]{0:T(256)S(1)} %iota_add_fusion), kind=kOutput, calls=%fused_computation.143 | convolution fusion | flops 24649728 | bytes 74752 | tf_op jit(solution)/shard_map/kc,wrc->wkr/dot_general | solution.py:90
  133.1 8.6 %fusion.80 = bf16[1,256,16]{1,2,0:T(8,128)(2,1)S(1)} fusion(bf16[16,2048]{1,0:T(8,128)(2,1)S(1)} %fusion.111, s32[256]{0:T(256)S(1)} %iota_add_fusion.1), kind=kOutput, calls=%fused_computation.140 | convolution fusion | flops 24649728 | bytes 74752 | tf_op jit(solution)/shard_map/kc,wrc->wkr/dot_general | solution.py:93
  141.7 8.0 %fusion.84 = bf16[1,256,16]{1,2,0:T(8,128)(2,1)S(1)} fusion(bf16[16,2048]{1,0:T(8,128)(2,1)S(1)} %fusion.111, s32[256]{0:T(256)S(1)} %iota_add_fusion.1), kind=kOutput, calls=%fused_computation.144 | convolution fusion | flops 24649728 | bytes 74752 | tf_op jit(solution)/shard_map/kc,wrc->wkr/dot_general | solution.py:90
  149.7 8.3 %fusion.81 = bf16[1,256,16]{1,2,0:T(8,128)(2,1)S(1)} fusion(bf16[16,2048]{1,0:T(8,128)(2,1)S(1)} %fusion.111, s32[256]{0:T(256)S(1)} %iota_add_fusion.2), kind=kOutput, calls=%fused_computation.141 | convolution fusion | flops 24649728 | bytes 74752 | tf_op jit(solution)/shard_map/kc,wrc->wkr/dot_general | solution.py:93
  158.0 8.0 %fusion.85 = bf16[1,256,16]{1,2,0:T(8,128)(2,1)S(1)} fusion(bf16[16,2048]{1,0:T(8,128)(2,1)S(1)} %fusion.111, s32[256]{0:T(256)S(1)} %iota_add_fusion.2), kind=kOutput, calls=%fused_computation.145 | convolution fusion | flops 24649728 | bytes 74752 | tf_op jit(solution)/shard_map/kc,wrc->wkr/dot_general | solution.py:90
  166.1 8.7 %fusion.86 = bf16[1,256,16]{1,2,0:T(8,128)(2,1)S(1)} fusion(bf16[16,2048]{1,0:T(8,128)(2,1)S(1)} %fusion.111), kind=kOutput, calls=%fused_computation.146 | convolution fusion | flops 24649728 | bytes 73728 | tf_op jit(solution)/shard_map/kc,wrc->wkr/dot_general | solution.py:90
  175.2 1.0 reshape.696
  176.2 16.4 %all-to-all-start.1 = ((bf16[128,2,128]{2,1,0:T(2,128)(2,1)}), bf16[128,2,128]{2,1,0:T(2,128)(2,1)S(1)}, u32[]{:S(2)}, u32[]{:S(2)}) async-start(bf16[128,2,128]{2,1,0:T(2,128)(2,1)} %reshape.696), calls=%async_computation.1 | async-start | bytes 131072 | tf_op jit(solution)/shard_map/all_to_all | solution.py:99
  192.8 14.1 %all-to-all-done.1 = bf16[128,2,128]{2,1,0:T(2,128)(2,1)S(1)} async-done(((bf16[128,2,128]{2,1,0:T(2,128)(2,1)}), bf16[128,2,128]{2,1,0:T(2,128)(2,1)S(1)}, u32[]{:S(2)}, u32[]{:S(2)}) %all-to-all-start.1) | async-done | bytes 65568 | tf_op jit(solution)/shard_map/all_to_all | solution.py:99
  207.5 0.8 reshape.673
  208.3 120.4 %while.24 = (s32[]{:T(128)}, f32[8,2048]{1,0:T(8,128)S(1)}, f32[8,2048]{1,0:T(8,128)S(1)}, f32[4,768]{1,0:T(4,128)S(1)}, bf16[16,2048]{1,0:T(8,128)(2,1)S(1)}, /...) while((s32[]{:T(128)}, f32[8,2048]{1,0:T(8,128)S(1)}, ...), condition=%wide.region_5.6_spmd.clone.clone, body=%wide.region_2.5_spmd.clone.clone.sunk | while | flops 98724360 | bytes 1034473 | solution.py:175
  230.1 7.8 %fusion.220 = f32[256,16]{0,1:T(8,128)S(1)} fusion(bf16[16,2048]{1,0:T(8,128)(2,1)S(1)} %get-tuple-element.510, s32[256]{0:T(256)S(1)} %get-tuple-element.469), kind=kOutput, calls=%fused_computation.16.clone.1 | convolution fusion | flops 24641536 | bytes 82944 | tf_op jit(solution)/shard_map/while/body/eval_jaxpr/dot_general | solution.py:142
  238.0 7.9 %fusion.219 = f32[256,16]{0,1:T(8,128)S(1)} fusion(bf16[16,2048]{1,0:T(8,128)(2,1)S(1)} %get-tuple-element.510, s32[256]{0:T(256)S(1)} %get-tuple-element.469), kind=kOutput, calls=%fused_computation.18.clone.1 | convolution fusion | flops 24641536 | bytes 82944 | tf_op jit(solution)/shard_map/while/body/eval_jaxpr/dot_general | solution.py:145
  246.0 7.9 %fusion.225 = f32[16,2048]{1,0:T(8,128)S(1)} fusion(s32[256]{0:T(256)S(1)} %get-tuple-element.469, bf16[256,8]{0,1:T(8,128)(2,1)S(1)} %get-tuple-element.478, bf16[256,8]{0,1:T(8,128)(2,1)S(1)} %get-tuple-element.479), kind=kOutput, calls=%fused_computation.17.clone.1 | convolution fusion | flops 24657920 | bytes 140288 | tf_op jit(solution)/shard_map/while/body/eval_jaxpr/dot_general | solution.py:167
  253.8 7.8 %fusion.224 = f32[16,2048]{1,0:T(8,128)S(1)} fusion(s32[256]{0:T(256)S(1)} %get-tuple-element.469, bf16[256,8]{0,1:T(8,128)(2,1)S(1)} %get-tuple-element.478, bf16[256,8]{0,1:T(8,128)(2,1)S(1)} %get-tuple-element.479), kind=kOutput, calls=%fused_computation.15.clone.1 | convolution fusion | flops 24657920 | bytes 140288 | tf_op jit(solution)/shard_map/while/body/eval_jaxpr/dot_general | solution.py:164
  261.8 7.8 %fusion.220 = f32[256,16]{0,1:T(8,128)S(1)} fusion(bf16[16,2048]{1,0:T(8,128)(2,1)S(1)} %get-tuple-element.510, s32[256]{0:T(256)S(1)} %get-tuple-element.469), kind=kOutput, calls=%fused_computation.16.clone.1 | convolution fusion | flops 24641536 | bytes 82944 | tf_op jit(solution)/shard_map/while/body/eval_jaxpr/dot_general | solution.py:142
  269.6 7.9 %fusion.219 = f32[256,16]{0,1:T(8,128)S(1)} fusion(bf16[16,2048]{1,0:T(8,128)(2,1)S(1)} %get-tuple-element.510, s32[256]{0:T(256)S(1)} %get-tuple-element.469), kind=kOutput, calls=%fused_computation.18.clone.1 | convolution fusion | flops 24641536 | bytes 82944 | tf_op jit(solution)/shard_map/while/body/eval_jaxpr/dot_general | solution.py:145
  277.6 7.9 %fusion.225 = f32[16,2048]{1,0:T(8,128)S(1)} fusion(s32[256]{0:T(256)S(1)} %get-tuple-element.469, bf16[256,8]{0,1:T(8,128)(2,1)S(1)} %get-tuple-element.478, bf16[256,8]{0,1:T(8,128)(2,1)S(1)} %get-tuple-element.479), kind=kOutput, calls=%fused_computation.17.clone.1 | convolution fusion | flops 24657920 | bytes 140288 | tf_op jit(solution)/shard_map/while/body/eval_jaxpr/dot_general | solution.py:167
  285.5 7.8 %fusion.224 = f32[16,2048]{1,0:T(8,128)S(1)} fusion(s32[256]{0:T(256)S(1)} %get-tuple-element.469, bf16[256,8]{0,1:T(8,128)(2,1)S(1)} %get-tuple-element.478, bf16[256,8]{0,1:T(8,128)(2,1)S(1)} %get-tuple-element.479), kind=kOutput, calls=%fused_computation.15.clone.1 | convolution fusion | flops 24657920 | bytes 140288 | tf_op jit(solution)/shard_map/while/body/eval_jaxpr/dot_general | solution.py:164
  293.5 7.8 %fusion.220 = f32[256,16]{0,1:T(8,128)S(1)} fusion(bf16[16,2048]{1,0:T(8,128)(2,1)S(1)} %get-tuple-element.510, s32[256]{0:T(256)S(1)} %get-tuple-element.469), kind=kOutput, calls=%fused_computation.16.clone.1 | convolution fusion | flops 24641536 | bytes 82944 | tf_op jit(solution)/shard_map/while/body/eval_jaxpr/dot_general | solution.py:142
  301.3 7.9 %fusion.219 = f32[256,16]{0,1:T(8,128)S(1)} fusion(bf16[16,2048]{1,0:T(8,128)(2,1)S(1)} %get-tuple-element.510, s32[256]{0:T(256)S(1)} %get-tuple-element.469), kind=kOutput, calls=%fused_computation.18.clone.1 | convolution fusion | flops 24641536 | bytes 82944 | tf_op jit(solution)/shard_map/while/body/eval_jaxpr/dot_general | solution.py:145
  309.3 7.9 %fusion.225 = f32[16,2048]{1,0:T(8,128)S(1)} fusion(s32[256]{0:T(256)S(1)} %get-tuple-element.469, bf16[256,8]{0,1:T(8,128)(2,1)S(1)} %get-tuple-element.478, bf16[256,8]{0,1:T(8,128)(2,1)S(1)} %get-tuple-element.479), kind=kOutput, calls=%fused_computation.17.clone.1 | convolution fusion | flops 24657920 | bytes 140288 | tf_op jit(solution)/shard_map/while/body/eval_jaxpr/dot_general | solution.py:167
  317.2 7.8 %fusion.224 = f32[16,2048]{1,0:T(8,128)S(1)} fusion(s32[256]{0:T(256)S(1)} %get-tuple-element.469, bf16[256,8]{0,1:T(8,128)(2,1)S(1)} %get-tuple-element.478, bf16[256,8]{0,1:T(8,128)(2,1)S(1)} %get-tuple-element.479), kind=kOutput, calls=%fused_computation.15.clone.1 | convolution fusion | flops 24657920 | bytes 140288 | tf_op jit(solution)/shard_map/while/body/eval_jaxpr/dot_general | solution.py:164
  328.7 0.7 copy.595
  329.5 1.1 reshape.698
  330.6 19.9 %all_to_all.35 = bf16[128,2,128]{2,1,0:T(2,128)(2,1)S(1)} all-to-all(bf16[128,2,128]{2,1,0:T(2,128)(2,1)S(1)} %reshape.698), channel_id=1, replica_groups=mesh['chain'=2,'slab'=128,'vis'=2] {'slab'}, dimensions={0} | all-to-all | bytes 131072 | tf_op jit(solution)/shard_map/all_to_all | solution.py:183
  350.5 1.2 reshape.699
  351.7 1.4 copy.599
  353.5 7.7 %fusion.87 = f32[16,2048]{1,0:T(8,128)S(1)} fusion(bf16[1,1024,16]{2,1,0:T(8,128)(2,1)S(1)} %bitcast.310), kind=kOutput, calls=%fused_computation.147 | convolution fusion | flops 24641536 | bytes 196608 | tf_op jit(solution)/shard_map/wkr,kc->wrc/dot_general | solution.py:191
  361.2 8.2 %convolution_subtract_fusion.3 = f32[16,2048]{1,0:T(8,128)S(1)} fusion(f32[16,2048]{1,0:T(8,128)S(1)} %fusion.87, bf16[1,1024,16]{2,1,0:T(8,128)(2,1)S(1)} %bitcast.306), kind=kOutput, calls=%fused_computation.88 | convolution fusion | flops 24674304 | bytes 327680 | tf_op jit(solution)/shard_map/wkr,kc->wrc/dot_general | solution.py:194
  369.4 8.0 %convolution_add_fusion.2 = f32[16,2048]{1,0:T(8,128)S(1)} fusion(f32[16,2048]{1,0:T(8,128)S(1)} %convolution_subtract_fusion.3, s32[256]{0:T(256)S(1)} %iota_add_fusion.2, bf16[1,1024,16]{2,1,0:T(8,128)(2,1)S(1)} %bitcast.311), kind=kOutput, calls=%fused_computation.87 | convolution fusion | flops 24674304 | bytes 328704 | tf_op jit(solution)/shard_map/wkr,kc->wrc/dot_general | solution.py:191
  377.4 7.9 %convolution_subtract_fusion.2 = f32[16,2048]{1,0:T(8,128)S(1)} fusion(f32[16,2048]{1,0:T(8,128)S(1)} %convolution_add_fusion.2, s32[256]{0:T(256)S(1)} %iota_add_fusion.2, bf16[1,1024,16]{2,1,0:T(8,128)(2,1)S(1)} %bitcast.307), kind=kOutput, calls=%fused_computation.86 | convolution fusion | flops 24674304 | bytes 328704 | tf_op jit(solution)/shard_map/wkr,kc->wrc/dot_general | solution.py:194
  385.3 8.0 %convolution_add_fusion.1 = f32[16,2048]{1,0:T(8,128)S(1)} fusion(f32[16,2048]{1,0:T(8,128)S(1)} %convolution_subtract_fusion.2, s32[256]{0:T(256)S(1)} %iota_add_fusion.1, bf16[1,1024,16]{2,1,0:T(8,128)(2,1)S(1)} %bitcast.312), kind=kOutput, calls=%fused_computation.85 | convolution fusion | flops 24674304 | bytes 328704 | tf_op jit(solution)/shard_map/wkr,kc->wrc/dot_general | solution.py:191
  393.3 8.3 %convolution_subtract_fusion.1 = f32[16,2048]{1,0:T(8,128)S(1)} fusion(f32[16,2048]{1,0:T(8,128)S(1)} %convolution_add_fusion.1, s32[256]{0:T(256)S(1)} %iota_add_fusion.1, bf16[1,1024,16]{2,1,0:T(8,128)(2,1)S(1)} %bitcast.308), kind=kOutput, calls=%fused_computation.84 | convolution fusion | flops 24674304 | bytes 328704 | tf_op jit(solution)/shard_map/wkr,kc->wrc/dot_general | solution.py:194
  401.6 7.8 %convolution_add_fusion = f32[16,2048]{1,0:T(8,128)S(1)} fusion(f32[16,2048]{1,0:T(8,128)S(1)} %convolution_subtract_fusion.1, s32[256]{0:T(256)S(1)} %iota_add_fusion, bf16[1,1024,16]{2,1,0:T(8,128)(2,1)S(1)} %bitcast.313), kind=kOutput, calls=%fused_computation.83 | convolution fusion | flops 24674304 | bytes 328704 | tf_op jit(solution)/shard_map/wkr,kc->wrc/dot_general | solution.py:191
  409.4 8.1 %slice_multiply_fusion.2 = (f32[1,16,2048]{2,1,0:T(8,128)S(1)}, bf16[1,16,2048]{2,1,0:T(8,128)(2,1)S(1)}) fusion(f32[2,16,2048]{2,1,0:T(8,128)S(1)} %fusion.98, f32[2,16,2048]{2,1,0:T(8,128)S(1)} %fusion.94, f32[16,2048]{1,0:T(8,128)S(1)} %convolution_add_fusion, s32[256]{0:T(256)S(1)} %iota_add_fusion, bf16[1,1024,16]{2,1,0:T(8,128)(2,1)S(1)} %bitcast.309), kind=kOutput, calls=%fused_computation.334 | convolution fusion | flops 24805376 | bytes 656384 | tf_op jit(solution)/shard_map/wkr,kc->wrc/dot_general | solution.py:194
  417.7 2.5 collective-permute-start.2
  420.3 9.0 %collective-permute-start.3 = (bf16[1,2,2048]{2,1,0:T(2,128)(2,1)S(1)}, bf16[1,2,2048]{2,1,0:T(2,128)(2,1)S(1)}, u32[]{:S(2)}, u32[]{:S(2)}) collective-permute-start(bf16[1,2,2048]{2,1,0:T(2,128)(2,1)S(1)} %get-tuple-element.420), channel_id=1, source_target_pairs={{2,0},{4,2},{6,4},{8,6},{10,8},{12,10},{14,12},{16,14},{18,16},{20... | collective-permute-start | bytes 24584 | tf_op jit(solution)/shard_map/ppermute | solution.py:22
  429.4 1.3 collective-permute-done.3
  430.7 0.8 fusion.103
  (200 shorter events, 80.5 us)
Async XLA Ops:
  1.0 107.0 %collective-permute-start = (bf16[2,2,2048]{2,1,0:T(2,128)(2,1)S(1)}, bf16[2,2,2048]{2,1,0:T(2,128)(2,1)S(1)}, u32[]{:S(2)}, u32[]{:S(2)}) collective-permute-start(bf16[2,2,2048]{2,1,0:T(2,128)(2,1)S(1)} %get-tuple-element.417), channel_id=1, source_target_pairs={{0,2},{2,4},{4,6},{6,8},{8,10},{10,12},{12,14},{14,16},{16,18},{18... | collective-permute-start | bytes 49160 | tf_op jit(solution)/shard_map/ppermute | solution.py:20
  4.5 103.5 %collective-permute-start.1 = (bf16[2,2,2048]{2,1,0:T(2,128)(2,1)S(1)}, bf16[2,2,2048]{2,1,0:T(2,128)(2,1)S(1)}, u32[]{:S(2)}, u32[]{:S(2)}) collective-permute-start(bf16[2,2,2048]{2,1,0:T(2,128)(2,1)S(1)} %get-tuple-element.418), channel_id=1, source_target_pairs={{2,0},{4,2},{6,4},{8,6},{10,8},{12,10},{14,12},{16,14},{18,16},{20... | collective-permute-start | bytes 49160 | tf_op jit(solution)/shard_map/ppermute | solution.py:22
  23.3 84.0 %copy-start = (f32[16,2048]{1,0:T(8,128)S(1)}, f32[16,2048]{1,0:T(8,128)}, u32[]{:S(2)}) copy-start(f32[16,2048]{1,0:T(8,128)} %param.11) | copy-start | bytes 393220
  23.3 84.0 %copy-start.1 = (f32[1,16,2048]{2,1,0:T(8,128)S(1)}, f32[1,16,2048]{2,1,0:T(8,128)}, u32[]{:S(2)}) copy-start(f32[1,16,2048]{2,1,0:T(8,128)} %param.10) | copy-start | bytes 393220
  97.9 78.3 %all-to-all-start = ((f32[128,4,1,6]{3,1,2,0:T(4,128)}), f32[128,4,1,6]{3,1,2,0:T(4,128)S(1)}, u32[]{:S(2)}, u32[]{:S(2)}) async-start(f32[128,4,1,6]{3,1,2,0:T(4,128)} %constant_dynamic-update-slice_fusion), calls=%async_computation | async-start | bytes 524288 | tf_op jit(solution)/shard_map/all_to_all | solution.py:126
  176.2 30.8 %all-to-all-start.1 = ((bf16[128,2,128]{2,1,0:T(2,128)(2,1)}), bf16[128,2,128]{2,1,0:T(2,128)(2,1)S(1)}, u32[]{:S(2)}, u32[]{:S(2)}) async-start(bf16[128,2,128]{2,1,0:T(2,128)(2,1)} %reshape.696), calls=%async_computation.1 | async-start | bytes 131072 | tf_op jit(solution)/shard_map/all_to_all | solution.py:99
  417.7 11.7 %collective-permute-start.2 = (bf16[1,2,2048]{2,1,0:T(2,128)(2,1)S(1)}, bf16[1,2,2048]{2,1,0:T(2,128)(2,1)S(1)}, u32[]{:S(2)}, u32[]{:S(2)}) collective-permute-start(bf16[1,2,2048]{2,1,0:T(2,128)(2,1)S(1)} %get-tuple-element.419), channel_id=1, source_target_pairs={{0,2},{2,4},{4,6},{6,8},{8,10},{10,12},{12,14},{14,16},{16,18},{18... | collective-permute-start | bytes 24584 | tf_op jit(solution)/shard_map/ppermute | solution.py:20
  420.3 10.4 %collective-permute-start.3 = (bf16[1,2,2048]{2,1,0:T(2,128)(2,1)S(1)}, bf16[1,2,2048]{2,1,0:T(2,128)(2,1)S(1)}, u32[]{:S(2)}, u32[]{:S(2)}) collective-permute-start(bf16[1,2,2048]{2,1,0:T(2,128)(2,1)S(1)} %get-tuple-element.420), channel_id=1, source_target_pairs={{2,0},{4,2},{6,4},{8,6},{10,8},{12,10},{14,12},{16,14},{18,16},{20... | collective-permute-start | bytes 24584 | tf_op jit(solution)/shard_map/ppermute | solution.py:22
